TPU v7x, 128 devices: a whole 4x4x4 slice. The times are simulated.
128 devices in a mesh: seq: 32 (over z, y, core), exp: 4 (over x).
Axes of the slice: x: 4, y: 4, z: 4, core: 2. Of those that a mesh axis runs over, the one named last changes fastest.
Arguments:
- residual_in: bfloat16 [16384, 2048], P(('seq', 'exp')), may hold values from -6 to 6
- query_input: bfloat16 [16384, 1024], P(('seq', 'exp')), may hold values from -6 to 6
- key_input: bfloat16 [16384, 1024], P(('seq', 'exp')), may hold values from -6 to 6
- value_input: bfloat16 [16384, 2048], P(('seq', 'exp')), may hold values from -6 to 6
- out_gate: bfloat16 [16384, 2048], P(('seq', 'exp')), may hold values from -6 to 6
- write_strength: float32 [16384, 16], P(('seq', 'exp')), may hold values from 0 to 2
- decay_rate: float32 [16384, 16], P(('seq', 'exp')), may hold values from 0 to 1
- head_gain: float32 [128], replicated, may hold values from 0.1 to 1.9
- out_proj: bfloat16 [2048, 2048], P(None, 'exp'), may hold values from -0.125 to 0.125
- post_gain: float32 [2048], replicated, may hold values from 0.1 to 1.9
- expert_ids: int32 [16384, 10], P(('seq', 'exp')), may hold values from 0 to 255, all different within a row; in each aligned block of 128 rows (0 to 127, 128 to 255, ...) at most 8 rows name the same one
- gate_weights: float32 [16384, 10], P(('seq', 'exp')), may hold values from 0.05 to 0.3
- expert_gate: bfloat16 [256, 2048, 512], P(('seq', 'exp')), may hold values from -0.125 to 0.125
- expert_up: bfloat16 [256, 2048, 512], P(('seq', 'exp')), may hold values from -0.125 to 0.125
- expert_down: bfloat16 [256, 512, 2048], P(('seq', 'exp')), may hold values from -0.25 to 0.25
Outputs:
- layer_out: bfloat16 [16384, 2048], P(('seq', 'exp'))
Inputs may be any that keep to these rules, and one draw needn't show every extreme that they name: `expert_ids`: each row names 10 different experts. Within the rows of one device (aligned blocks of 128 rows) no expert is named more than 8 times, and in every draw some expert is named exactly 8 times within one device's rows.
All inputs are finite; a program needn't handle non-finite values.
Results may differ from a plain program's by a relative error of at most 0.011.
Values may be sent and summed in bfloat16 or wider, within the bound.
A program may use at most 256 MiB of HBM per device.

v0:
```python
import jax
import jax.numpy as jnp
from jax import lax
from jax.sharding import PartitionSpec as P

D = 2048
HK = 8
GROUP_VALUE_HEADS = 16
DK = 128
DV = 128
CH = 64
TOP = 10


largest_value = lax.Precision.HIGHEST


def prefix_2(array, axis, combine, identity):
    devices, index = (lax.axis_size(axis), lax.axis_index(axis))
    everything = jax.tree.map(lambda part: lax.all_gather(part, axis), array)
    start = jax.tree.map(
        lambda part, zero: jnp.broadcast_to(jnp.asarray(zero, part.dtype), part.shape),
        array,
        identity,
    )

    def hop(k, before):
        reached = k < index
        new = combine(before, jax.tree.map(lambda part: part[k], everything))
        return jax.tree.map(lambda a, b: jnp.where(reached, a, b), new, before)

    return lax.fori_loop(0, devices, hop, start)


def broadcast(array, axis, root):
    mine = lax.axis_index(axis) == root
    return lax.psum(jnp.where(mine, array, jnp.zeros_like(array)), axis)


def unit_rows(block):
    return block * lax.rsqrt(jnp.sum(block * block, axis=-1, keepdims=True) + 1e-06)


def block_terms(query_block, key_block, value_block, strength, rate):
    block_len = key_block.shape[1]
    width = key_block.shape[2]
    logs = jnp.cumsum(-rate, axis=1)
    log_gap = logs[:, :, None] - logs[:, None, :]
    row_ids = jnp.arange(block_len)[:, None]
    column_ids = jnp.arange(block_len)[None, :]
    inclusive = (row_ids >= column_ids)[None]
    strict = (row_ids > column_ids)[None]
    ratio = jnp.where(inclusive, jnp.exp(jnp.where(inclusive, log_gap, 0.0)), 0.0)
    key_gram = jnp.einsum("htd,hsd->hts", key_block, key_block, precision=largest_value)
    system = jnp.where(strict, ratio * key_gram, 0.0) * strength[:, :, None] + jnp.eye(
        block_len, dtype=jnp.float32
    )
    growth = jnp.exp(logs)
    newest_value = jax.scipy.linalg.solve_triangular(
        system, strength[:, :, None] * value_block, lower=True, unit_diagonal=True
    )
    key_matrix = jax.scipy.linalg.solve_triangular(
        system, (strength * growth)[:, :, None] * key_block, lower=True, unit_diagonal=True
    )
    mixed_query = ratio * jnp.einsum(
        "htd,hsd->hts", query_block, key_block, precision=largest_value
    )
    faded_key = key_block * jnp.exp(logs[:, -1:] - logs)[:, :, None]
    transition_matrix = growth[:, -1][:, None, None] * jnp.eye(
        width, dtype=jnp.float32
    ) - jnp.einsum("hck,hcj->hkj", faded_key, key_matrix, precision=largest_value)
    increment_term = jnp.einsum("btx,btw->bxw", faded_key, newest_value, precision=largest_value)
    return (
        query_block * growth[:, :, None],
        mixed_query,
        newest_value,
        key_matrix,
        transition_matrix,
        increment_term,
    )


def block_output(passed_state, rescaled_query, mixed_query, newest_value, key_matrix):
    state_update = newest_value - jnp.einsum(
        "lxw,lwp->lxp", key_matrix, passed_state, precision=largest_value
    )
    return jnp.einsum(
        "lxw,lwp->lxp", rescaled_query, passed_state, precision=largest_value
    ) + jnp.einsum("xib,xbp->xip", mixed_query, state_update, precision=largest_value)


def compose(earlier, later):
    merged_map = jnp.einsum("hij,hjk->hik", later[0], earlier[0], precision=largest_value)
    merged_add = (
        jnp.einsum("hij,hjk->hik", later[0], earlier[1], precision=largest_value) + later[1]
    )
    return (merged_map, merged_add)


def prepare(query_input, key_input, value_input, write_strength, decay_rate):
    tok_rows = key_input.shape[0]
    blocks_here = tok_rows // CH
    head_group = GROUP_VALUE_HEADS // HK
    query_unit = unit_rows(query_input.reshape(tok_rows, HK, DK).astype(jnp.float32)) * DK ** (-0.5)
    key_unit = unit_rows(key_input.reshape(tok_rows, HK, DK).astype(jnp.float32))
    query_unit = jnp.repeat(query_unit, head_group, axis=1)
    key_unit = jnp.repeat(key_unit, head_group, axis=1)
    value_heads = value_input.reshape(tok_rows, GROUP_VALUE_HEADS, DV).astype(jnp.float32)

    def blocked(array):
        shaped = array.reshape((blocks_here, CH) + array.shape[1:])
        return jnp.swapaxes(shaped, 1, 2)

    return jax.vmap(block_terms)(
        blocked(query_unit),
        blocked(key_unit),
        blocked(value_heads),
        blocked(write_strength),
        blocked(decay_rate),
    )


def finish_core(outputs, out_gate, head_gain):
    tok_rows = out_gate.shape[0]
    recurrent = jnp.swapaxes(outputs, 1, 2).reshape(tok_rows, GROUP_VALUE_HEADS, DV)
    inv_rms = lax.rsqrt(jnp.mean(recurrent * recurrent, axis=2, keepdims=True) + 1e-06)
    gate_act = jax.nn.silu(out_gate.reshape(tok_rows, GROUP_VALUE_HEADS, DV).astype(jnp.float32))
    return (
        (recurrent * inv_rms * head_gain * gate_act)
        .astype(jnp.bfloat16)
        .reshape(tok_rows, GROUP_VALUE_HEADS * DV)
    )


def post_norm(hidden_state, post_gain):
    widened = hidden_state.astype(jnp.float32)
    return (
        widened * lax.rsqrt(jnp.mean(widened * widened, axis=1, keepdims=True) + 1e-06) * post_gain
    ).astype(jnp.bfloat16)


def slot_index(expert_ids, experts, capacity):
    flat_ids = expert_ids.reshape(-1)
    onehot = (flat_ids[:, None] == jnp.arange(experts, dtype=jnp.int32)[None, :]).astype(jnp.int32)
    before = jnp.cumsum(onehot, axis=0) - onehot
    return flat_ids * capacity + jnp.sum(before * onehot, axis=1)


def expert_ffn(received, expert_gate, expert_up, expert_down):
    gate_part = jnp.einsum(
        "secd,edf->secf", received, expert_gate, preferred_element_type=jnp.float32
    )
    up_part = jnp.einsum("secd,edf->secf", received, expert_up, preferred_element_type=jnp.float32)
    inner = (jax.nn.silu(gate_part) * up_part).astype(jnp.bfloat16)
    return jnp.einsum(
        "secf,efd->secd", inner, expert_down, preferred_element_type=jnp.float32
    ).astype(jnp.bfloat16)


def shards(
    residual_in,
    query_input,
    key_input,
    value_input,
    out_gate,
    write_strength,
    decay_rate,
    head_gain,
    out_proj,
    post_gain,
    expert_ids,
    gate_weights,
    expert_gate,
    expert_up,
    expert_down,
):
    tok_rows = residual_in.shape[0]
    pieces = prepare(query_input, key_input, value_input, write_strength, decay_rate)
    identity = (
        jnp.broadcast_to(jnp.eye(DK, dtype=jnp.float32), (GROUP_VALUE_HEADS, DK, DK)),
        jnp.zeros((GROUP_VALUE_HEADS, DK, DV), jnp.float32),
    )

    def fold_step(carry_maps, item):
        return (compose(carry_maps, item), None)

    own_map, _ = lax.scan(fold_step, identity, (pieces[4], pieces[5]))
    inner_prefix = prefix_2(own_map, "exp", compose, identity)
    through = compose(inner_prefix, own_map)
    group_map = (
        broadcast(through[0], "exp", lax.axis_size("exp") - 1),
        broadcast(through[1], "exp", lax.axis_size("exp") - 1),
    )
    outer_prefix = prefix_2(group_map, "seq", compose, identity)
    prefix = compose(outer_prefix, inner_prefix)

    def emit_block(passed_state, item):
        rescaled_query, mixed_query, newest_value, key_matrix, transition_matrix, increment_term = (
            item
        )
        emitted = block_output(passed_state, rescaled_query, mixed_query, newest_value, key_matrix)
        moved_forward = (
            jnp.einsum("aip,ape->aie", transition_matrix, passed_state, precision=largest_value)
            + increment_term
        )
        return (moved_forward, emitted)

    _, outputs = lax.scan(emit_block, prefix[1], pieces)
    core_out = finish_core(outputs, out_gate, head_gain)
    mixer_out = jnp.dot(
        core_out,
        lax.all_gather(out_proj, "exp", axis=1, tiled=True),
        preferred_element_type=jnp.float32,
    )
    hidden_state = (residual_in.astype(jnp.float32) + mixer_out).astype(jnp.bfloat16)
    normed = post_norm(hidden_state, post_gain)
    devices = lax.axis_size(("seq", "exp"))
    local_experts = expert_gate.shape[0]
    experts = local_experts * devices
    capacity = max(2, tok_rows * TOP * 8 // (5 * experts))
    slots = slot_index(expert_ids, experts, capacity)
    send_buffer = (
        jnp.zeros((experts * capacity, D), jnp.bfloat16)
        .at[slots]
        .set(jnp.repeat(normed, TOP, axis=0))
    )
    send_buffer = send_buffer.reshape(devices, local_experts, capacity, D)
    seq_count = lax.axis_size("seq")
    exp_count = lax.axis_size("exp")
    sectioned = send_buffer.reshape(seq_count, exp_count, local_experts, capacity, D)
    received = lax.all_to_all(
        lax.all_to_all(sectioned, "seq", split_axis=0, concat_axis=0, tiled=True),
        "exp",
        split_axis=1,
        concat_axis=1,
        tiled=True,
    )
    result = expert_ffn(
        received.reshape(devices, local_experts, capacity, D), expert_gate, expert_up, expert_down
    )
    result = result.reshape(seq_count, exp_count, local_experts, capacity, D)
    returned = lax.all_to_all(
        lax.all_to_all(result, "seq", split_axis=0, concat_axis=0, tiled=True),
        "exp",
        split_axis=1,
        concat_axis=1,
        tiled=True,
    )
    picked = (
        returned.reshape(experts * capacity, D)[slots].reshape(tok_rows, TOP, D).astype(jnp.float32)
    )
    routed = jnp.sum(gate_weights[:, :, None] * picked, axis=1)
    return (hidden_state.astype(jnp.float32) + routed).astype(jnp.bfloat16)


def solution(mesh):
    placed = (
        P(("seq", "exp"), None),
        P(("seq", "exp"), None),
        P(("seq", "exp"), None),
        P(("seq", "exp"), None),
        P(("seq", "exp"), None),
        P(("seq", "exp"), None),
        P(("seq", "exp"), None),
        P(),
        P(None, "exp"),
        P(),
        P(("seq", "exp"), None),
        P(("seq", "exp"), None),
        P(("seq", "exp"), None, None),
        P(("seq", "exp"), None, None),
        P(("seq", "exp"), None, None),
    )
    return jax.shard_map(
        shards, mesh=mesh, in_specs=placed, out_specs=P(("seq", "exp"), None), check_vma=False
    )
```

profile of v0, /device:TPU:1, one launch (start us, length us, event | category | flops | bytes accessed | tf_op | source)
XLA Modules:
  0.0 1405.2 jit_solution(9212975366905402052)
XLA Ops:
  12.8 158.5 %custom-call.7 = f32[2,16,1,64,64]{3,4,2,1,0:T(8,128)} custom-call(f32[2,16,1,64,64]{4,3,2,1,0:T(8,128)S(1)} %fusion.69), custom_call_target="InvertDiagBlocksLowerTriangular" | custom-call | tf_op jit(solution)/shard_map/vmap(jit(_solve_triangular))/vmap()/triangular_solve | solution.py:62
  177.4 4.8 fusion.89
  182.2 5.1 multiply_subtract_fusion
  187.5 11.8 while.56
  201.1 50.5 %all-gather.14.cloned.1.call-done = f32[64,128,128]{2,1,0:T(8,128)} async-done(((f32[16,128,128]{2,1,0:T(8,128)}), f32[64,128,128]{2,1,0:T(8,128)}) %all-gather.14.cloned.1.call-update) | async-done | bytes 4194320 | tf_op jit(solution)/shard_map/all_gather | solution.py:20
  251.7 50.2 %all-gather.16.cloned.1.call-done = f32[64,128,128]{2,1,0:T(8,128)} async-done(((f32[16,128,128]{2,1,0:T(8,128)}), f32[64,128,128]{2,1,0:T(8,128)}) %all-gather.16.cloned.1.call-update) | async-done | bytes 4194320 | tf_op jit(solution)/shard_map/all_gather | solution.py:20
  302.9 34.2 %while.57 = (s32[]{:T(128)}, f32[16,128,128]{2,1,0:T(8,128)}, f32[16,128,128]{2,1,0:T(8,128)}, s32[]{:T(128)}, f32[4,16,128,128]{3,2,1,0:T(8,128)}, /*index=5*/f32[4,16,128,128]{3,2,1,0:T(8,128)}, s32[]{:T(128)}, s32[]{:T(128)}) while((s32[]{:T(128)}, f32[16,128,128]{2,1,0:T(8,128)}, f32[16,128,128]{2,1,0:T(8,128)}, s32[]{:T(128)}, ...), condition=%wide.region_5.7_spmd.clone, body=%wide.region_4.6_spmd.clone.sunk | while | flops 806617088 | bytes 17828996 | solution.py:32
  343.2 59.1 %all-reduce.3.cloned.1.call-done = (f32[1,16,128,128]{3,2,1,0:T(8,128)}, f32[1,16,128,128]{3,2,1,0:T(8,128)}) async-done(((f32[1,16,128,128]{3,2,1,0:T(8,128)}, f32[1,16,128,128]{3,2,1,0:T(8,128)}), (f32[1,16,128,128]{3,2,1,0:T(8,128)}, f32[1,16,128,128]{3,2,1,0:T(8,128)})) %all-reduce.3.cloned.1.call-update) | async-done | bytes 2097168 | tf_op jit(solution)/shard_map/psum | solution.py:37
  418.3 100.3 %all-gather.10.cloned.1.call-done = f32[32,16,128,128]{3,2,1,0:T(8,128)} async-done(((f32[1,16,128,128]{3,2,1,0:T(8,128)}), f32[32,16,128,128]{3,2,1,0:T(8,128)}) %all-gather.10.cloned.1.call-update) | async-done | bytes 33554448 | tf_op jit(solution)/shard_map/all_gather | solution.py:20
  518.7 115.2 %all-gather.8.cloned.1.call-done = f32[32,16,128,128]{3,2,1,0:T(8,128)} async-done(((f32[1,16,128,128]{3,2,1,0:T(8,128)}), f32[32,16,128,128]{3,2,1,0:T(8,128)}) %all-gather.8.cloned.1.call-update) | async-done | bytes 33554448 | tf_op jit(solution)/shard_map/all_gather | solution.py:20
  633.8 161.1 %while.58 = (s32[]{:T(128)}, f32[16,128,128]{2,1,0:T(8,128)}, s32[]{:T(128)}, f32[32,16,128,128]{3,2,1,0:T(8,128)}, f32[32,16,128,128]{3,2,1,0:T(8,128)}, /*index=5*/s32[]{:T(128)}, s32[]{:T(128)}) while((s32[]{:T(128)}, f32[16,128,128]{2,1,0:T(8,128)}, s32[]{:T(128)}, f32[32,16,128,128]{3,2,1,0:T(8,128)}, ...), condition=%wide.region_9.11_spmd.clone, body=%wide.region_8.10_spmd.clone.sunk | while | flops 403701760 | bytes 7342687 | solution.py:32
  798.6 18.1 %while.55 = (s32[]{:T(128)}, f32[16,128,128]{2,1,0:T(8,128)}, f32[2,16,64,128]{3,2,1,0:T(8,128)}, f32[2,16,128,128]{3,2,1,0:T(8,128)S(1)}, f32[2,16,128,128]{3,2...) while((s32[]{:T(128)}, f32[16,128,128]{2,1,0:T(8,128)}, ...), condition=%wide.region_12.14_spmd, body=%wide.region_11.13_spmd.sunk | while | flops 906493952 | bytes 36179188 | solution.py:208
  820.7 5.5 multiply_reduce_fusion.1
  830.7 9.8 reshape.181
  840.6 16.0 %scatter_custom_fusion = bf16[2048,2048]{1,0:T(8,128)(2,1)} fusion(s32[1280]{0:T(1024)S(1)} %fusion.101, bf16[1280,2048]{1,0:T(8,128)(2,1)} %reshape.181, bf16[]{:T(256)} %constant.117.clone.1), kind=kCustom, calls=%fused_computation.68 | custom fusion | bytes 8389120 | tf_op jit(solution)/shard_map/scatter | solution.py:225
  856.6 101.2 %all_to_all.20 = bf16[32,4,2,8,2048]{4,3,2,1,0:T(8,128)(2,1)} all-to-all(bf16[32,4,2,8,2048]{4,3,2,1,0:T(8,128)(2,1)} %bitcast.238), channel_id=1, replica_groups=mesh['seq'=32,'exp'=4] {'seq'}, dimensions={0} | all-to-all | bytes 16777216 | tf_op jit(solution)/shard_map/all_to_all | solution.py:232
  957.8 8.3 copy.110
  966.0 97.6 %all_to_all.21 = bf16[32,4,2,8,2048]{4,3,2,0,1:T(8,128)(2,1)S(1)} all-to-all(bf16[32,4,2,8,2048]{4,3,2,0,1:T(8,128)(2,1)} %copy.110), channel_id=1, replica_groups=mesh['seq'=32,'exp'=4] {'exp'}, dimensions={1} | all-to-all | bytes 16777216 | tf_op jit(solution)/shard_map/all_to_all | solution.py:231
  1063.7 17.4 %copy.111 = bf16[32,4,2,8,2048]{4,1,0,3,2:T(4,128)(2,1)} copy(bf16[32,4,2,8,2048]{4,3,2,0,1:T(8,128)(2,1)S(1)} %all_to_all.21) | data formatting | bytes 16777216 | tf_op jit(solution)/shard_map/all_to_all | solution.py:231
  1081.1 12.5 reshape.162
  1093.6 11.0 fusion.46
  1104.6 15.4 %convert_bitcast_fusion = bf16[128,2,8,2048]{3,0,2,1:T(8,128)(2,1)} fusion(bf16[2,512,2048]{2,1,0:T(8,128)(2,1)} %param.39, f32[2,128,8,512]{3,1,2,0:T(8,128)} %fusion.46, bf16[128,2,8,2048]{3,0,2,1:T(8,128)(2,1)} %reshape.162, bf16[2,2048,512]{2,1,0:T(8,128)(2,1)} %param.37), kind=kOutput, calls=%fused_computation.55 | convolution fusion | flops 8600420352 | bytes 29360128 | tf_op jit(solution)/shard_map/secf,efd->secd/dot_general | solution.py:155
  1120.0 13.1 reshape.163
  1133.1 5.8 copy.112
  1138.9 100.9 %all_to_all.22 = bf16[32,4,2,8,2048]{4,1,3,2,0:T(4,128)(2,1)} all-to-all(bf16[32,4,2,8,2048]{4,1,3,2,0:T(4,128)(2,1)S(1)} %copy.112), channel_id=1, replica_groups=mesh['seq'=32,'exp'=4] {'seq'}, dimensions={0} | all-to-all | bytes 16777216 | tf_op jit(solution)/shard_map/all_to_all | solution.py:243
  1239.8 11.3 copy.113
  1251.1 5.8 all-to-all-start.3
  1257.0 93.4 %all-to-all-done.3 = bf16[32,4,2,8,2048]{4,0,3,2,1:T(8,128)(2,1)} async-done(((bf16[32,4,2,8,2048]{4,0,3,2,1:T(8,128)(2,1)}), bf16[32,4,2,8,2048]{4,0,3,2,1:T(8,128)(2,1)}, u32[]{:S(2)}, u32[]{:S(2)}) %all-to-all-start.3) | async-done | bytes 8388640 | tf_op jit(solution)/shard_map/all_to_all | solution.py:242
  1350.4 11.3 copy.114
  1361.7 15.3 %gather_fusion = bf16[1280,2048]{1,0:T(8,128)(2,1)} fusion(bf16[2048,2048]{1,0:T(8,128)(2,1)} %bitcast.237, s32[2048]{0:T(1024)S(1)} %pad_clamp_fusion), kind=kCustom, calls=%fused_computation | custom fusion | bytes 10490880 | tf_op jit(solution)/shard_map/gather | solution.py:250
  1377.0 10.6 reshape.167
  1387.6 9.6 multiply_reduce_fusion
  (253 shorter events, 275.0 us)
Async XLA Ops:
  6.5 407.5 %copy-start = (f32[128]{0:T(128)S(1)}, f32[128]{0:T(128)}, u32[]{:S(2)}) copy-start(f32[128]{0:T(128)} %param.32) | copy-start | bytes 1540
  6.5 245.1 %all-gather.14.cloned.1.call-start = ((), (), s32[]{:S(2)}) async-start(), calls=%async_computation.7 | async-start | bytes 5242880 | tf_op jit(solution)/shard_map/all_gather | solution.py:20
  10.0 161.4 %copy-start.19 = (bf16[128,2048]{1,0:T(8,128)(2,1)S(1)}, bf16[128,2048]{1,0:T(8,128)(2,1)}, u32[]{:S(2)}) copy-start(bf16[128,2048]{1,0:T(8,128)(2,1)} %param.28) | copy-start | bytes 1572868
  10.8 161.6 %copy-start.12 = (f32[128,8,2,128]{3,0,2,1:T(8,128)}, f32[128,8,2,128]{3,0,2,1:T(8,128)S(1)}, u32[]{:S(2)}) copy-start(f32[128,8,2,128]{3,0,2,1:T(8,128)S(1)} %broadcast_in_dim.72) | copy-start | bytes 3145732
  172.3 4.1 copy-start.14
  174.3 7.9 copy-start.8
  200.3 101.6 %all-gather.16.cloned.1.call-start = ((), (), s32[]{:S(2)}) async-start(), calls=%async_computation.8 | async-start | bytes 5242880 | tf_op jit(solution)/shard_map/all_gather | solution.py:20
  201.1 201.2 %all-reduce.3.cloned.1.call-start = ((), (), s32[]{:S(2)}) async-start(), calls=%async_computation.9 | async-start | bytes 4194304 | tf_op jit(solution)/shard_map/psum | solution.py:37
  302.9 34.2 %copy-start.3 = (f32[16,128,128]{2,1,0:T(8,128)S(1)}, f32[16,128,128]{2,1,0:T(8,128)}, u32[]{:S(2)}) copy-start(f32[16,128,128]{2,1,0:T(8,128)} %copy-done.2) | copy-start | bytes 3145732
  302.9 5.2 copy-start.5
  311.5 5.1 copy-start.5
  320.1 5.1 copy-start.5
  328.6 5.1 copy-start.5
  341.0 62.5 %copy-start.21 = (s32[128,10]{0,1:T(8,128)S(1)}, s32[128,10]{0,1:T(8,128)}, u32[]{:S(2)}) copy-start(s32[128,10]{0,1:T(8,128)} %param.35) | copy-start | bytes 15364
  341.0 62.9 %copy-start.20 = (bf16[128,1024]{1,0:T(8,128)(2,1)S(1)}, bf16[128,1024]{1,0:T(8,128)(2,1)}, u32[]{:S(2)}) copy-start(bf16[128,1024]{1,0:T(8,128)(2,1)} %param.26) | copy-start | bytes 786436
  343.2 175.5 %all-gather.10.cloned.1.call-start = ((), (), s32[]{:S(2)}) async-start(), calls=%async_computation.5 | async-start | bytes 34603008 | tf_op jit(solution)/shard_map/all_gather | solution.py:20
  402.3 231.5 %all-gather.8.cloned.1.call-start = ((), (), s32[]{:S(2)}) async-start(), calls=%async_computation.4 | async-start | bytes 34603008 | tf_op jit(solution)/shard_map/all_gather | solution.py:20
  402.9 417.4 %all-gather.12.cloned.1.call-start = ((), (), s32[]{:S(2)}) async-start(), calls=%async_computation.6 | async-start | bytes 10485760 | tf_op jit(solution)/shard_map/all_gather | solution.py:212
  408.9 6.6 copy-start.13
  633.8 161.1 %copy-start.7 = (f32[16,128,128]{2,1,0:T(8,128)S(1)}, f32[16,128,128]{2,1,0:T(8,128)}, u32[]{:S(2)}) copy-start(f32[16,128,128]{2,1,0:T(8,128)} %get-tuple-element.287) | copy-start | bytes 3145732
  798.6 4.1 copy-start.11
  798.6 4.8 copy-start.10
  798.6 4.8 copy-start.17
  798.6 6.9 copy-start.4
  807.6 4.1 copy-start.11
  807.6 4.8 copy-start.10
  807.6 4.8 copy-start.17
  807.6 6.9 copy-start.4
  820.6 5.5 copy-start.22
  1251.1 5.8 copy-start.23
  1251.1 99.3 %all-to-all-start.3 = ((bf16[32,4,2,8,2048]{4,0,3,2,1:T(8,128)(2,1)}), bf16[32,4,2,8,2048]{4,0,3,2,1:T(8,128)(2,1)}, u32[]{:S(2)}, u32[]{:S(2)}) async-start(bf16[32,4,2,8,2048]{4,0,3,2,1:T(8,128)(2,1)} %copy.113), calls=%async_computation.3 | async-start | bytes 16777216 | tf_op jit(solution)/shard_map/all_to_all | solution.py:242
  1387.6 10.5 copy-start.1
  (9 other events, 18.3 us)
Sparse Core Ops, SparseCore 0:
  200.4 51.1 all-gather.13
  253.3 48.5 all-gather.15
  343.3 58.9 all-reduce.2
  404.4 114.1 all-gather.9
  520.8 113.0 all-gather.7
  635.4 81.6 all-gather.11
where the time goes:
time: 1410 us
  waiting for transfers between devices  471 us (33%)
  blocking collectives  300 us (21%)
  matrix products  232 us (16%)
  local copies, waits for them, and re-layouts  201 us (14%)
  other arithmetic  181 us (13%)
  between operations  14.3 us (1%)
    all_gather x4, waiting for transfers between devices, prefix_2(): everything = jax.tree.map(lambda part: lax.all_gather(part, axis), array)  316 us
    another operation x4, other arithmetic, block_terms(): jax.scipy.linalg.solve_triangular(system, (strength * growth)[:, :, None]...  159 us
    dot_general x40, matrix products, compose(): jnp.einsum('hij,hjk->hik', later[0], earlier[1], precision=largest_value)  151 us
    all_to_all x1, blocking collectives, shards(): lax.all_to_all(sectioned, 'seq', split_axis=0, concat_axis=0, tiled=True)  101 us
    all_to_all x1, blocking collectives, shards(): lax.all_to_all(result, 'seq', split_axis=0, concat_axis=0, tiled=True)  101 us
    all_to_all x1, blocking collectives, shards(): lax.all_to_all(lax.all_to_all(sectioned, 'seq', split_axis=0, concat_axis...  97.6 us
    all_to_all x1, waiting for transfers between devices, shards(): lax.all_to_all(lax.all_to_all(result, 'seq', split_axis=0, concat_axis=0,...  93.4 us
    psum x1, waiting for transfers between devices, broadcast(): return lax.psum(jnp.where(mine, array, jnp.zeros_like(array)), axis)  59.1 us
  transfers between devices with their start and end apart: 7, of which 6 were waited for; matrix products, arithmetic and copies ran while one was open for 14% of the time, Pallas kernels for 0%

commit v1 on v0

v1 whole, which is shorter than its diff:
```python
from functools import partial

import jax
import jax.numpy as jnp
from jax import lax
from jax.experimental import pallas as pl
from jax.experimental.pallas import tpu as pltpu
from jax.sharding import PartitionSpec as P

D = 2048
HK = 8
HV = 16
DK = 128
DV = 128
TOP = 10
GROUP = 16

F32 = jnp.float32
BF16 = jnp.bfloat16
MESH = pl.DeviceIdType.MESH


def mm(a, b):
    return jnp.dot(a, b, preferred_element_type=F32)


def mm_t(a, b):
    return lax.dot_general(a, b, (((1,), (1,)), ((), ())), preferred_element_type=F32)


def split(x):
    high = x.astype(BF16)
    return high, (x - high.astype(F32)).astype(BF16)


def mm3(a, b):
    return mm(a[0], b[0]) + (mm(a[0], b[1]) + mm(a[1], b[0]))


def iota(axis):
    return lax.broadcasted_iota(jnp.int32, (128, 128), axis)


def rows_of(row):
    return jnp.broadcast_to(row, (128, 128))


def unit_inverse(lower):
    row, col = iota(0), iota(1)
    eye = jnp.where(row == col, 1.0, 0.0)
    inverse = eye - jnp.where((row >> 1) == (col >> 1), lower, 0.0)
    for level in range(1, 7):
        mask = ((row >> (level + 1)) == (col >> (level + 1))) & ((row >> level) != (col >> level))
        part = split(jnp.where(mask, lower, 0.0))
        blocks = split(inverse)
        inverse = inverse - mm3(blocks, split(mm3(part, blocks)))
    return inverse


def mixer_kernel(
    seq_size,
    exp_size,
    q_ref,
    k_ref,
    v_ref,
    gate_ref,
    rate_ref,
    beta_ref,
    gain_ref,
    out_ref,
    logs,
    local_out,
    query_high,
    query_low,
    maps,
    maps_in,
    prefix,
    groups_in,
    states,
    states_in,
    send1,
    recv1,
    send2,
    recv2,
    send3,
    recv3,
):
    lines = GROUP // exp_size
    groups = seq_size // lines
    seq, exp = lax.axis_index("seq"), lax.axis_index("exp")
    group = seq // lines
    rank = (seq % lines) * exp_size + exp

    def device(of_group, of_rank):
        return (of_group * lines + of_rank // exp_size, of_rank % exp_size)

    barrier = pltpu.get_barrier_semaphore()

    def greet_rank(step, carry):
        pl.semaphore_signal(barrier, inc=1, device_id=device(group, lax.rem(rank + step, GROUP)), device_id_type=MESH)
        return carry

    def greet_group(step, carry):
        pl.semaphore_signal(barrier, inc=1, device_id=device(lax.rem(group + step, groups), rank), device_id_type=MESH)
        return carry

    lax.fori_loop(1, GROUP, greet_rank, 0)
    lax.fori_loop(1, groups, greet_group, 0)
    pl.semaphore_wait(barrier, GROUP - 1 + groups - 1)

    row, col = iota(0), iota(1)
    upto = jnp.where(row <= col, 1.0, 0.0).astype(BF16)
    rate = rate_ref[...]
    first, rest = split(rate)
    last = (rate - first.astype(F32) - rest.astype(F32)).astype(BF16)
    logs[...] = -(mm(first, upto) + (mm(rest, upto) + mm(last, upto)))

    def map_copy(head, to):
        return pltpu.make_async_remote_copy(
            src_ref=maps.at[head],
            dst_ref=maps_in.at[to],
            send_sem=send1.at[head],
            recv_sem=recv1.at[to],
            device_id=device(group, head),
            device_id_type=MESH,
        )

    def map_keep(head, to):
        return pltpu.make_async_copy(maps.at[head], maps_in.at[to], recv1.at[to])

    def key_head(kh, carry):
        columns = pl.ds(pl.multiple_of(kh * DK, DK), DK)
        k_raw, q_raw = k_ref[:, columns], q_ref[:, columns]
        k_wide, q_wide = k_raw.astype(F32), q_raw.astype(F32)
        k_inv = lax.rsqrt(jnp.sum(k_wide * k_wide, axis=1, keepdims=True) + 1e-6)
        q_inv = lax.rsqrt(jnp.sum(q_wide * q_wide, axis=1, keepdims=True) + 1e-6) * DK ** (-0.5)
        k_inv = jnp.broadcast_to(k_inv, (128, 128))
        k_inv_row = k_inv.T
        k_t = k_wide.T.astype(BF16)
        gram = mm_t(k_raw, k_raw) * k_inv * k_inv_row
        mixed = mm_t(q_raw, k_raw) * q_inv * k_inv_row
        for part in range(HV // HK):
            h = kh * (HV // HK) + part
            head_columns = pl.ds(pl.multiple_of(h * DV, DV), DV)
            log_row = rows_of(logs[pl.ds(h, 1), :])
            log_col = log_row.T
            beta_row = rows_of(beta_ref[pl.ds(h, 1), :])
            beta_col = beta_row.T
            ratio = jnp.where(row >= col, jnp.exp(jnp.where(row >= col, log_col - log_row, 0.0)), 0.0)
            inverse = unit_inverse(jnp.where(row > col, ratio * gram, 0.0) * beta_col)
            v_raw = v_ref[:, head_columns]
            weights = split(inverse * beta_row)
            newest = mm(weights[0], v_raw) + mm(weights[1], v_raw)
            weights = split(inverse * (beta_row * jnp.exp(log_row) * k_inv_row))
            key_matrix = mm(weights[0], k_raw) + mm(weights[1], k_raw)
            log_last = jnp.broadcast_to(logs[pl.ds(h, 1), 127:128], (128, 128))
            fade = k_inv * jnp.exp(log_last - log_col)
            side = split(key_matrix * fade)
            moved = mm(k_t, side[0]) + mm(k_t, side[1])
            maps[h, :, :DK] = jnp.where(row == col, jnp.exp(log_last), 0.0) - moved
            side = split(newest * fade)
            maps[h, :, DK:] = mm(k_t, side[0]) + mm(k_t, side[1])

            @pl.when(h != rank)
            def _():
                map_copy(h, rank).start()

            @pl.when(h == rank)
            def _():
                map_keep(h, rank).start()

            mix = split(mixed * ratio)
            local_out[h] = mm3(mix, split(newest))
            effective = split(q_wide * q_inv * jnp.exp(log_col) - mm3(mix, split(key_matrix)))
            query_high[h] = effective[0]
            query_low[h] = effective[1]
        return carry

    lax.fori_loop(0, HK, key_head, 0)

    map_keep(0, 0).wait()
    prefix[0] = maps_in[0]

    def chain(index, carry):
        map_keep(index, index).wait()
        step = split(maps_in[index, :, :DK])
        before = prefix[index - 1]
        prefix[index, :, :DK] = mm3(step, split(before[:, :DK]))
        prefix[index, :, DK:] = mm3(step, split(before[:, DK:])) + maps_in[index, :, DK:]
        return carry

    lax.fori_loop(1, GROUP, chain, 0)

    def group_copy(to, source):
        return pltpu.make_async_remote_copy(
            src_ref=prefix.at[GROUP - 1],
            dst_ref=groups_in.at[source],
            send_sem=send2.at[to],
            recv_sem=recv2.at[source],
            device_id=device(to, rank),
            device_id_type=MESH,
        )

    def send_group(to, carry):
        group_copy(to, group).start()
        return carry

    lax.fori_loop(group + 1, groups, send_group, 0)

    def enter(source, state):
        group_copy(group, source).wait_recv()
        return mm3(split(groups_in[source, :, :DK]), split(state)) + groups_in[source, :, DK:]

    entering = split(lax.fori_loop(0, group, enter, jnp.zeros((DK, DV), F32)))

    def state_copy(to, head):
        return pltpu.make_async_remote_copy(
            src_ref=states.at[to],
            dst_ref=states_in.at[head],
            send_sem=send3.at[to],
            recv_sem=recv3.at[head],
            device_id=device(group, to),
            device_id_type=MESH,
        )

    def state_keep(to, head):
        return pltpu.make_async_copy(states.at[to], states_in.at[head], recv3.at[head])

    def give(to):
        @pl.when(to != rank)
        def _():
            state_copy(to, rank).start()

        @pl.when(to == rank)
        def _():
            state_keep(to, rank).start()

    states[0] = entering[0]
    give(0)

    def spread(index, carry):
        moved = mm3(split(prefix[index - 1, :, :DK]), entering) + prefix[index - 1, :, DK:]
        states[index] = moved.astype(BF16)
        give(index)
        return carry

    lax.fori_loop(1, GROUP, spread, 0)

    gain = gain_ref[...]

    def finish(h, carry):
        columns = pl.ds(pl.multiple_of(h * DV, DV), DV)
        gate = gate_ref[:, columns].astype(F32)
        scale = gain * (gate / (1.0 + jnp.exp(-gate)))
        state_keep(h, h).wait()
        state = states_in[h]
        out = local_out[h] + (mm(query_high[h], state) + mm(query_low[h], state))
        inv_rms = lax.rsqrt(jnp.sum(out * out, axis=1, keepdims=True) * (1.0 / DV) + 1e-6)
        out_ref[:, columns] = (out * inv_rms * scale).astype(BF16)
        return carry

    lax.fori_loop(0, HV, finish, 0)

    def drain(index, carry):
        @pl.when(index != rank)
        def _():
            map_copy(index, rank).wait_send()
            state_copy(index, rank).wait_send()

        return carry

    lax.fori_loop(0, GROUP, drain, 0)

    def drain_group(to, carry):
        group_copy(to, group).wait_send()
        return carry

    lax.fori_loop(group + 1, groups, drain_group, 0)


def mixer_core(query, key, value, gate, strength, rate, head_gain):
    seq_size, exp_size = lax.axis_size("seq"), lax.axis_size("exp")
    groups = seq_size * exp_size // GROUP
    tokens = query.shape[0]
    vmem = pl.BlockSpec(memory_space=pltpu.VMEM)
    return pl.pallas_call(
        partial(mixer_kernel, seq_size, exp_size),
        out_shape=jax.ShapeDtypeStruct((tokens, HV * DV), BF16),
        in_specs=[vmem] * 7,
        out_specs=vmem,
        scratch_shapes=[
            pltpu.VMEM((HV, tokens), F32),
            pltpu.VMEM((HV, tokens, DV), F32),
            pltpu.VMEM((HV, tokens, DK), BF16),
            pltpu.VMEM((HV, tokens, DK), BF16),
            pltpu.VMEM((HV, DK, DK + DV), F32),
            pltpu.VMEM((GROUP, DK, DK + DV), F32),
            pltpu.VMEM((GROUP, DK, DK + DV), F32),
            pltpu.VMEM((groups, DK, DK + DV), F32),
            pltpu.VMEM((GROUP, DK, DV), BF16),
            pltpu.VMEM((HV, DK, DV), BF16),
            pltpu.SemaphoreType.DMA((HV,)),
            pltpu.SemaphoreType.DMA((GROUP,)),
            pltpu.SemaphoreType.DMA((groups,)),
            pltpu.SemaphoreType.DMA((groups,)),
            pltpu.SemaphoreType.DMA((GROUP,)),
            pltpu.SemaphoreType.DMA((HV,)),
        ],
        compiler_params=pltpu.CompilerParams(
            collective_id=0, has_side_effects=True, vmem_limit_bytes=32 * 1024 * 1024
        ),
        cost_estimate=pl.CostEstimate(flops=8_000_000_000, bytes_accessed=4_000_000, transcendentals=0),
    )(query, key, value, gate, rate.T, strength.T, head_gain.reshape(1, DV))


def post_norm(hidden_state, post_gain):
    widened = hidden_state.astype(F32)
    return (widened * lax.rsqrt(jnp.mean(widened * widened, axis=1, keepdims=True) + 1e-6) * post_gain).astype(BF16)


def slot_tables(expert_ids, gate_weights, experts, capacity):
    tokens = expert_ids.shape[0]
    named = expert_ids.T[:, None, :] == jnp.arange(experts, dtype=jnp.int32)[None, :, None]
    weight = jnp.sum(jnp.where(named, gate_weights.T[:, None, :], 0.0), axis=0)
    chosen = jnp.any(named, axis=0)
    earlier = jnp.arange(tokens)[:, None] < jnp.arange(tokens)[None, :]
    before = jnp.dot(chosen.astype(BF16), earlier.astype(BF16), preferred_element_type=F32).astype(jnp.int32)
    before = jnp.where(chosen, before, -1)
    here = before[:, None, :] == jnp.arange(capacity, dtype=jnp.int32)[None, :, None]
    pick = here.astype(BF16).reshape(experts * capacity, tokens)
    mix = jnp.where(here, weight[:, None, :], 0.0).reshape(experts * capacity, tokens)
    return pick, mix


def shards(
    residual_in,
    query_input,
    key_input,
    value_input,
    out_gate,
    write_strength,
    decay_rate,
    head_gain,
    out_proj,
    post_gain,
    expert_ids,
    gate_weights,
    expert_gate,
    expert_up,
    expert_down,
):
    tokens = residual_in.shape[0]
    devices = lax.axis_size(("seq", "exp"))
    local_experts = expert_gate.shape[0]
    experts = local_experts * devices
    capacity = max(2, tokens * TOP * 8 // (5 * experts))
    all_proj = lax.all_gather(out_proj, "exp", axis=1, tiled=True)
    pick, mix = slot_tables(expert_ids, gate_weights, experts, capacity)
    core_out = mixer_core(query_input, key_input, value_input, out_gate, write_strength, decay_rate, head_gain)
    mixer_out = jnp.dot(core_out, all_proj, preferred_element_type=F32)
    hidden_state = (residual_in.astype(F32) + mixer_out).astype(BF16)
    normed = post_norm(hidden_state, post_gain)
    send = jnp.dot(pick, normed, preferred_element_type=F32).astype(BF16)
    send = send.reshape(devices, local_experts * capacity, D)
    received = lax.all_to_all(send, ("seq", "exp"), split_axis=0, concat_axis=0, tiled=True)
    received = received.reshape(devices, local_experts, capacity, D)
    results = []
    for e in range(local_experts):
        block = received[:, e].reshape(devices * capacity, D)
        gate_part = jnp.dot(block, expert_gate[e], preferred_element_type=F32)
        up_part = jnp.dot(block, expert_up[e], preferred_element_type=F32)
        inner = (gate_part / (1.0 + jnp.exp(-gate_part)) * up_part).astype(BF16)
        result = jnp.dot(inner, expert_down[e], preferred_element_type=F32).astype(BF16)
        results.append(result.reshape(devices, 1, capacity, D))
    result = jnp.concatenate(results, axis=1).reshape(devices, local_experts * capacity, D)
    returned = lax.all_to_all(result, ("seq", "exp"), split_axis=0, concat_axis=0, tiled=True)
    returned = returned.reshape(experts * capacity, D)
    mix_high = mix.astype(BF16)
    mix_low = (mix - mix_high.astype(F32)).astype(BF16)
    both = lax.dot_general(
        jnp.concatenate([mix_high, mix_low], axis=1),
        returned,
        (((0,), (0,)), ((), ())),
        preferred_element_type=F32,
    )
    routed = both[:tokens] + both[tokens:]
    return (hidden_state.astype(F32) + routed).astype(BF16)


def solution(mesh):
    both = ("seq", "exp")
    placed = (
        P(both, None),
        P(both, None),
        P(both, None),
        P(both, None),
        P(both, None),
        P(both, None),
        P(both, None),
        P(),
        P(None, "exp"),
        P(),
        P(both, None),
        P(both, None),
        P(both, None, None),
        P(both, None, None),
        P(both, None, None),
    )
    return jax.shard_map(shards, mesh=mesh, in_specs=placed, out_specs=P(both, None), check_vma=False)
```

time: 1410 us -> 397 us (0.28)
  waiting for transfers between devices: 471 us -> 136 us
  local copies, waits for them, and re-layouts: 201 us -> 6.17 us
  blocking collectives: 300 us -> 107 us
  matrix products: 232 us -> 42.1 us
  other arithmetic: 181 us -> 10.4 us
  Pallas kernels: 0 us -> 75.1 us
    all_gather x5 -> x1, waiting for transfers between devices: 316 us -> 33.5 us  [shards(): all_proj = lax.all_gather(out_proj, 'exp', axis=1, tiled=True)]
    all_to_all x3 -> x1, blocking collectives: 300 us -> 107 us  [shards(): lax.all_to_all(send, ('seq', 'exp'), split_axis=0, concat_axis=0, tiled=T...]
    dot_general x62 -> x8, matrix products: 228 us -> 42.1 us  [the longest x2 21.2 us: shards(): jnp.dot(inner, expert_down[e], preferred_element_type=F32).astype(BF16)]
    another operation x8 -> x0, other arithmetic: 161 us -> none  [the longest x4 159 us: block_terms(): jax.scipy.linalg.solve_triangular(system, (strength * growth)[:, :, None]...]
    pallas_call x0 -> x1, Pallas kernels: none -> 75.1 us  [mixer_core(): pl.pallas_call(partial(mixer_kernel, seq_size, exp_size), out_shape=jax.S...]
    psum x1 -> x0, waiting for transfers between devices: 59.1 us -> none  [broadcast(): return lax.psum(jnp.where(mine, array, jnp.zeros_like(array)), axis)]
    while x74 -> x0, local copies, waits for them, and re-layouts: 52.6 us -> none
    all_to_all x4 -> x0, local copies, waits for them, and re-layouts: 48.2 us -> none  [the longest x1 17.4 us: shards(): lax.all_to_all(lax.all_to_all(sectioned, 'seq', split_axis=0, concat_axis...]
  transfers between devices with their start and end apart: 7 -> 2, of which waited for: 6 -> 2; matrix products, arithmetic and copies ran while one was open for 14% -> 1% of each run, Pallas kernels for 0% -> 19%
where the time goes in v1:
time: 397 us; the launch traced here: 396 us
  waiting for transfers between devices  136 us (34%)
  blocking collectives  107 us (27%)
  Pallas kernels  75.1 us (19%)
  matrix products  42.1 us (11%)
  between operations  13.5 us (3%)
  other arithmetic  10.4 us (3%)
  local copies, waits for them, and re-layouts  6.17 us (2%)
  starting transfers between devices  5.37 us (1%)
    all_to_all x1, blocking collectives, shards(): lax.all_to_all(send, ('seq', 'exp'), split_axis=0, concat_axis=0, tiled=T...  107 us
    all_to_all x1, waiting for transfers between devices, shards(): lax.all_to_all(result, ('seq', 'exp'), split_axis=0, concat_axis=0, tiled...  102 us
    pallas_call x1, Pallas kernels, mixer_core(): pl.pallas_call(partial(mixer_kernel, seq_size, exp_size), out_shape=jax.S...  75.1 us
    all_gather x1, waiting for transfers between devices, shards(): all_proj = lax.all_gather(out_proj, 'exp', axis=1, tiled=True)  33.5 us
    dot_general x2, matrix products, shards(): jnp.dot(inner, expert_down[e], preferred_element_type=F32).astype(BF16)  21.2 us
  transfers between devices with their start and end apart: 2, of which 2 were waited for; matrix products, arithmetic and copies ran while one was open for 1% of the time, Pallas kernels for 19%

profile of v1, /device:TPU:1, one launch (start us, length us, event | category | flops | bytes accessed | tf_op | source)
XLA Modules:
  0.0 395.9 jit_solution(6428110841140978727)
XLA Ops:
  6.5 0.0 all-gather.2.cloned.1.call-start
  6.5 0.7 all-gather.2.cloned.1.call-update
  7.3 0.1 eq.40
  7.4 0.9 fusion.22
  8.3 0.2 fusion.27
  8.4 1.0 copy-done
  9.5 1.0 copy-done.1
  10.5 0.9 copy-done.2
  11.5 0.9 copy-done.3
  12.4 0.7 copy-done.4
  13.1 0.7 copy-done.5
  13.8 0.7 copy-done.6
  14.5 75.1 %shard_map.145 = bf16[128,2048]{1,0:T(8,128)(2,1)S(1)} custom-call(bf16[128,1024]{1,0:T(8,128)(2,1)S(1)} %copy-done.2, bf16[128,1024]{1,0:T(8,128)(2,1)S(1)} %copy-done.3, bf16[128,2048]{1,0:T(8,128)(2,1)S(1)} %copy-done, bf16[128,2048]{1,0:T(8,128)(2,1)S(1)} %copy-done.1, f32[16,128]{1,0:T(8,128)S(1)} %bitcast.83, f32[16,128]{1,0:T(8,128)S(1)} %bitcast.84, ...), custom_call_target="tpu_custom_call" | custom-call | flops 8000000000 | bytes 4000000 | tf_op jit(solution)/shard_map/pallas_call | solution.py:286
  89.6 0.0 copy-start.11
  89.6 33.5 %all-gather.2.cloned.1.call-done = bf16[2048,2048]{1,0:T(8,128)(2,1)} async-done(((bf16[2048,512]{1,0:T(8,128)(2,1)}), bf16[2048,2048]{1,0:T(8,128)(2,1)}) %all-gather.2.cloned.1.call-update) | async-done | bytes 8388624 | tf_op jit(solution)/shard_map/all_gather | solution.py:357
  123.1 4.8 %multiply_reduce_fusion = (f32[128]{0:T(128)S(1)}, f32[128,2048]{1,0:T(8,128)S(1)}) fusion(bf16[128,2048]{1,0:T(8,128)(2,1)S(1)} %shard_map.145, bf16[2048,2048]{1,0:T(8,128)(2,1)} %all-gather.2.cloned.1.call-done, bf16[128,2048]{1,0:T(8,128)(2,1)S(1)} %copy-done.8), kind=kOutput, calls=%fused_computation.47 | convolution fusion | flops 1075314560 | bytes 10486272 | tf_op jit(solution)/shard_map/dot_general | solution.py:360
  127.9 2.7 convolution_convert_fusion
  130.6 0.0 copy-start.12
  130.6 107.0 %all_to_all.10 = bf16[128,16,2048]{2,1,0:T(8,128)(2,1)S(1)} all-to-all(bf16[128,16,2048]{2,1,0:T(8,128)(2,1)S(1)} %bitcast.86), channel_id=1, replica_groups=mesh['seq'=32,'exp'=4] {'seq','exp'}, dimensions={0} | all-to-all | bytes 16777216 | tf_op jit(solution)/shard_map/all_to_all | solution.py:365
  237.6 3.8 fusion.1
  241.4 0.0 copy-done.7
  241.5 3.7 fusion.3
  245.1 10.6 %convert_bitcast_fusion.1 = bf16[128,1,8,2048]{3,2,1,0:T(8,128)(2,1)} fusion(bf16[2,512,2048]{2,1,0:T(8,128)(2,1)} %param.29, f32[1024,512]{1,0:T(8,128)} %fusion.1, bf16[2,2048,512]{2,1,0:T(8,128)(2,1)} %param.28, bf16[128,2,8,2048]{3,2,1,0:T(8,128)(2,1)} %bitcast.89), kind=kOutput, calls=%fused_computation.5 | convolution fusion | flops 4299685888 | bytes 14680064 | tf_op jit(solution)/shard_map/dot_general | solution.py:373
  255.7 10.6 %convert_bitcast_fusion = bf16[128,1,8,2048]{3,2,1,0:T(8,128)(2,1)} fusion(bf16[2,512,2048]{2,1,0:T(8,128)(2,1)} %param.29, f32[1024,512]{1,0:T(8,128)} %fusion.3, bf16[2,2048,512]{2,1,0:T(8,128)(2,1)} %param.28, bf16[128,2,8,2048]{3,2,1,0:T(8,128)(2,1)} %bitcast.90), kind=kOutput, calls=%fused_computation.4 | convolution fusion | flops 4299685888 | bytes 14680064 | tf_op jit(solution)/shard_map/dot_general | solution.py:373
  266.3 7.5 %maximum_bitcast_fusion = bf16[128,16,2048]{2,1,0:T(8,128)(2,1)} fusion(bf16[128,1,8,2048]{3,2,1,0:T(8,128)(2,1)} %convert_bitcast_fusion, bf16[128,1,8,2048]{3,2,1,0:T(8,128)(2,1)} %convert_bitcast_fusion.1), kind=kLoop, calls=%fused_computation | loop fusion | flops 4194304 | bytes 16777216 | tf_op jit(solution)/shard_map/reshape | solution.py:375
  273.8 5.4 %all-to-all-start.1 = ((bf16[128,16,2048]{2,1,0:T(8,128)(2,1)}), bf16[128,16,2048]{2,1,0:T(8,128)(2,1)}, u32[]{:S(2)}, u32[]{:S(2)}) async-start(bf16[128,16,2048]{2,1,0:T(8,128)(2,1)} %maximum_bitcast_fusion), calls=%async_computation.1 | async-start | bytes 16777216 | tf_op jit(solution)/shard_map/all_to_all | solution.py:376
  279.2 0.1 select_reduce_fusion
  279.4 0.4 fusion.35
  279.8 0.4 fusion.36
  280.3 102.1 %all-to-all-done.1 = bf16[128,16,2048]{2,1,0:T(8,128)(2,1)} async-done(((bf16[128,16,2048]{2,1,0:T(8,128)(2,1)}), bf16[128,16,2048]{2,1,0:T(8,128)(2,1)}, u32[]{:S(2)}, u32[]{:S(2)}) %all-to-all-start.1) | async-done | bytes 8388640 | tf_op jit(solution)/shard_map/all_to_all | solution.py:376
  382.4 5.7 %fusion.30 = f32[256,2048]{1,0:T(8,128)S(1)} fusion(bf16[2048,2048]{1,0:T(8,128)(2,1)} %bitcast.22, bf16[2048,128]{1,0:T(8,128)(2,1)S(1)} %fusion.36, bf16[2048,128]{1,0:T(8,128)(2,1)S(1)} %fusion.35), kind=kOutput, calls=%fused_computation.35 | convolution fusion | flops 2149580800 | bytes 11534336 | tf_op jit(solution)/shard_map/dot_general | solution.py:380
  388.1 1.0 fusion.29
  (18 shorter events, 0.0 us)
Async XLA Ops:
  6.5 116.6 %all-gather.2.cloned.1.call-start = ((), (), s32[]{:S(2)}) async-start(), calls=%async_computation.2 | async-start | bytes 10485760 | tf_op jit(solution)/shard_map/all_gather | solution.py:357
  8.4 1.0 copy-start
  9.5 1.0 copy-start.1
  10.5 0.9 copy-start.2
  11.5 0.9 copy-start.3
  12.4 0.7 copy-start.4
  13.1 0.7 copy-start.5
  13.8 0.7 copy-start.6
  14.5 108.6 %copy-start.8 = (bf16[128,2048]{1,0:T(8,128)(2,1)S(1)}, bf16[128,2048]{1,0:T(8,128)(2,1)}, u32[]{:S(2)}) copy-start(bf16[128,2048]{1,0:T(8,128)(2,1)} %param.15) | copy-start | bytes 1572868
  89.6 38.3 %copy-start.11 = (f32[2048]{0:T(1024)S(1)}, f32[2048]{0:T(1024)}, u32[]{:S(2)}) copy-start(f32[2048]{0:T(1024)} %param.24) | copy-start | bytes 24580
  130.6 107.0 %copy-start.12 = (bf16[2,2048,512]{2,1,0:T(8,128)(2,1)S(1)}, bf16[2,2048,512]{2,1,0:T(8,128)(2,1)}, u32[]{:S(2)}) copy-start(bf16[2,2048,512]{2,1,0:T(8,128)(2,1)} %param.27) | copy-start | bytes 12582916
  237.6 3.9 copy-start.7
  273.8 5.4 %copy-start.9 = (s32[128,10]{0,1:T(8,128)S(1)}, s32[128,10]{0,1:T(8,128)}, u32[]{:S(2)}) copy-start(s32[128,10]{0,1:T(8,128)} %param.25) | copy-start | bytes 15364
  273.8 5.4 %copy-start.10 = (f32[128,10]{0,1:T(8,128)S(1)}, f32[128,10]{0,1:T(8,128)}, u32[]{:S(2)}) copy-start(f32[128,10]{0,1:T(8,128)} %param.26) | copy-start | bytes 15364
  273.8 108.5 %all-to-all-start.1 = ((bf16[128,16,2048]{2,1,0:T(8,128)(2,1)}), bf16[128,16,2048]{2,1,0:T(8,128)(2,1)}, u32[]{:S(2)}, u32[]{:S(2)}) async-start(bf16[128,16,2048]{2,1,0:T(8,128)(2,1)} %maximum_bitcast_fusion), calls=%async_computation.1 | async-start | bytes 16777216 | tf_op jit(solution)/shard_map/all_to_all | solution.py:376
Sparse Core Ops, SparseCore 0:
  9.0 114.0 all-gather.1

commit v2 on v1

v2 whole, which is shorter than its diff:
```python
from functools import partial

import jax
import jax.numpy as jnp
from jax import lax
from jax.experimental import pallas as pl
from jax.experimental.pallas import tpu as pltpu
from jax.sharding import PartitionSpec as P

D = 2048
HK = 8
HV = 16
DK = 128
DV = 128
TOP = 10
TOGETHER = 1
GROUP = 16

F32 = jnp.float32
BF16 = jnp.bfloat16
MESH = pl.DeviceIdType.MESH


def mm(a, b):
    return jnp.dot(a, b, preferred_element_type=F32)


def mm_t(a, b):
    return lax.dot_general(a, b, (((1,), (1,)), ((), ())), preferred_element_type=F32)


def split(x):
    high = x.astype(BF16)
    return high, (x - high.astype(F32)).astype(BF16)


def mm3(a, b):
    return mm(a[0], b[0]) + (mm(a[0], b[1]) + mm(a[1], b[0]))


def iota(axis):
    return lax.broadcasted_iota(jnp.int32, (128, 128), axis)


def rows_of(row):
    return jnp.broadcast_to(row, (128, 128))


def unit_inverse(lower):
    row, col = iota(0), iota(1)
    eye = jnp.where(row == col, 1.0, 0.0)
    inverse = eye - jnp.where((row >> 1) == (col >> 1), lower, 0.0)
    for level in range(1, 7):
        mask = ((row >> (level + 1)) == (col >> (level + 1))) & ((row >> level) != (col >> level))
        part = split(jnp.where(mask, lower, 0.0))
        blocks = split(inverse)
        inverse = inverse - mm3(blocks, split(mm3(part, blocks)))
    return inverse


def mixer_kernel(
    seq_size,
    exp_size,
    stride,
    q_hbm,
    k_hbm,
    v_hbm,
    gate_hbm,
    residual_hbm,
    proj_hbm,
    rate_ref,
    beta_ref,
    gain_ref,
    post_gain_ref,
    hidden_ref,
    normed_ref,
    q_ref,
    k_ref,
    v_ref,
    gate_ref,
    residual_ref,
    proj,
    core_out,
    logs,
    local_out,
    query_high,
    query_low,
    maps,
    adds,
    maps_in,
    adds_in,
    prefix,
    prefix_add,
    last_add,
    groups_in,
    groups_add,
    states,
    states_in,
    load,
    send1,
    recv1,
    send2,
    recv2,
    send3,
    recv3,
    proj_send,
    proj_recv,
):
    lines = GROUP // exp_size
    groups = seq_size // lines
    seq, exp = lax.axis_index("seq"), lax.axis_index("exp")
    group = seq // lines
    rank = (seq % lines) * exp_size + exp

    loads = [
        pltpu.make_async_copy(source, target, load.at[number])
        for number, (source, target) in enumerate(
            [
                (k_hbm, k_ref),
                (q_hbm, q_ref),
                (v_hbm, v_ref),
                (gate_hbm, gate_ref),
                (residual_hbm, residual_ref),
                (proj_hbm, proj.at[exp]),
            ]
        )
    ]
    for copy in loads:
        copy.start()

    def device(of_group, of_rank):
        return (of_group * lines + of_rank // exp_size, of_rank % exp_size)

    core = seq % 2
    spot = (seq // stride) % 4

    def ring_seq(shift):
        return seq + ((spot + shift) % 4 - spot) * stride

    def ring_exp(shift):
        return lax.rem(exp + shift, 4)

    partner = (seq + 1 - 2 * core, exp)
    rows = proj_hbm.shape[0] // 8
    half = rows // 2

    def piece(x_shift, spot_shift, begin, size):
        row = pl.multiple_of(core * (4 * rows) + (spot + spot_shift) % 4 * rows + begin, half)
        return proj.at[ring_exp(x_shift), pl.ds(row, size)]

    counter = [0]

    def proj_copy(ref, recv_index, to, source=None):
        number = counter[0]
        counter[0] += 1
        return pltpu.make_async_remote_copy(
            src_ref=ref if source is None else source,
            dst_ref=ref,
            send_sem=proj_send.at[number],
            recv_sem=proj_recv.at[recv_index],
            device_id=to,
            device_id_type=MESH,
        )

    def landing(ref, recv_index):
        return pltpu.make_async_copy(ref, ref, proj_recv.at[recv_index])

    own = proj_hbm.at[pl.ds(pl.multiple_of(core * (4 * rows) + spot * rows, half), rows)]
    mine = piece(0, 0, 0, rows)
    right, left = (seq, ring_exp(1)), (seq, ring_exp(3))
    above, below = (ring_seq(1), exp), (ring_seq(3), exp)
    x_first = [proj_copy(mine, 0, right, own), proj_copy(mine, 1, left, own)]
    x_second = [proj_copy(piece(3, 0, 0, half), 2, right), proj_copy(piece(1, 0, half, half), 3, left)]
    x_landing = [
        landing(piece(3, 0, 0, rows), 0),
        landing(piece(1, 0, 0, rows), 1),
        landing(piece(2, 0, 0, half), 2),
        landing(piece(2, 0, half, half), 3),
    ]
    shifts = (3, 1, 2)
    z_first, z_second, z_landing, across, across_landing = [], [], [], [], []
    for number, shift in enumerate(shifts):
        at = 4 + 4 * number
        z_first.append(
            [proj_copy(piece(shift, 0, 0, rows), at, above), proj_copy(piece(shift, 0, 0, rows), at + 1, below)]
        )
        z_second.append(
            [proj_copy(piece(shift, 3, 0, half), at + 2, above), proj_copy(piece(shift, 1, half, half), at + 3, below)]
        )
        z_landing.append(
            [
                landing(piece(shift, 3, 0, rows), at),
                landing(piece(shift, 1, 0, rows), at + 1),
                landing(piece(shift, 2, 0, half), at + 2),
                landing(piece(shift, 2, half, half), at + 3),
            ]
        )
        across.append([proj_copy(piece(shift, n, 0, rows), 16 + 4 * number + n, partner) for n in range(4)])
        other = (1 - core) * (4 * rows)
        across_landing.append(
            [
                landing(
                    proj.at[
                        ring_exp(shift), pl.ds(pl.multiple_of(other + (spot + n) % 4 * rows, half), rows)
                    ],
                    16 + 4 * number + n,
                )
                for n in range(4)
            ]
        )

    barrier = pltpu.get_barrier_semaphore()

    def greet(to):
        pl.semaphore_signal(barrier, inc=1, device_id=to, device_id_type=MESH)

    def greet_rank(step, carry):
        greet(device(group, lax.rem(rank + step, GROUP)))
        return carry

    def greet_group(step, carry):
        greet(device(lax.rem(group + step, groups), rank))
        return carry

    lax.fori_loop(1, GROUP, greet_rank, 0)
    lax.fori_loop(1, groups, greet_group, 0)
    for to in (right, left, above, below, partner):
        greet(to)
    pl.semaphore_wait(barrier, GROUP - 1 + groups - 1 + 5)

    for copy in x_first:
        copy.start()

    row, col = iota(0), iota(1)
    upto = jnp.where(row <= col, 1.0, 0.0).astype(BF16)
    rate = rate_ref[...]
    first, rest = split(rate)
    last = (rate - first.astype(F32) - rest.astype(F32)).astype(BF16)
    logs[...] = -(mm(first, upto) + (mm(rest, upto) + mm(last, upto)))
    for copy in loads[:3]:
        copy.wait()

    def map_copies(head, to):
        return [
            pltpu.make_async_remote_copy(
                src_ref=source.at[head],
                dst_ref=target.at[to],
                send_sem=send1.at[number, head],
                recv_sem=recv1.at[number, to],
                device_id=device(group, head),
                device_id_type=MESH,
            )
            for number, (source, target) in enumerate([(maps, maps_in), (adds, adds_in)])
        ]

    def map_keeps(head, to):
        return [
            pltpu.make_async_copy(maps.at[head], maps_in.at[to], recv1.at[0, to]),
            pltpu.make_async_copy(adds.at[head], adds_in.at[to], recv1.at[1, to]),
        ]

    def key_head(kh):
        columns = pl.ds(pl.multiple_of(kh * DK, DK), DK)
        k_raw, q_raw = k_ref[:, columns], q_ref[:, columns]
        k_wide, q_wide = k_raw.astype(F32), q_raw.astype(F32)
        k_inv = lax.rsqrt(jnp.sum(k_wide * k_wide, axis=1, keepdims=True) + 1e-6)
        q_inv = lax.rsqrt(jnp.sum(q_wide * q_wide, axis=1, keepdims=True) + 1e-6) * DK ** (-0.5)
        k_inv = jnp.broadcast_to(k_inv, (128, 128))
        k_inv_row = k_inv.T
        k_t = k_wide.T.astype(BF16)
        gram = mm_t(k_raw, k_raw) * k_inv * k_inv_row
        mixed = mm_t(q_raw, k_raw) * q_inv * k_inv_row
        for part in range(HV // HK):
            h = kh * (HV // HK) + part
            head_columns = pl.ds(pl.multiple_of(h * DV, DV), DV)
            log_row = rows_of(logs[pl.ds(h, 1), :])
            log_col = log_row.T
            beta_row = rows_of(beta_ref[pl.ds(h, 1), :])
            beta_col = beta_row.T
            ratio = jnp.where(row >= col, jnp.exp(jnp.where(row >= col, log_col - log_row, 0.0)), 0.0)
            inverse = unit_inverse(jnp.where(row > col, ratio * gram, 0.0) * beta_col)
            v_raw = v_ref[:, head_columns]
            weights = split(inverse * beta_row)
            newest = mm(weights[0], v_raw) + mm(weights[1], v_raw)
            weights = split(inverse * (beta_row * jnp.exp(log_row) * k_inv_row))
            key_matrix = mm(weights[0], k_raw) + mm(weights[1], k_raw)
            log_last = jnp.broadcast_to(logs[pl.ds(h, 1), 127:128], (128, 128))
            fade = k_inv * jnp.exp(log_last - log_col)
            side = split(key_matrix * fade)
            moved = mm(k_t, side[0]) + mm(k_t, side[1])
            maps[h] = jnp.where(row == col, jnp.exp(log_last), 0.0) - moved
            side = split(newest * fade)
            adds[h] = (mm(k_t, side[0]) + mm(k_t, side[1])).astype(BF16)
            mix = split(mixed * ratio)
            local_out[h] = mm3(mix, split(newest))
            effective = split(q_wide * q_inv * jnp.exp(log_col) - mm3(mix, split(key_matrix)))
            query_high[h] = effective[0]
            query_low[h] = effective[1]

    def key_heads(step, carry):
        for part in range(TOGETHER):
            key_head(step * TOGETHER + part)
        for part in range(TOGETHER * (HV // HK)):
            h = step * (TOGETHER * (HV // HK)) + part

            @pl.when(h != rank)
            def _():
                for copy in map_copies(h, rank):
                    copy.start()

            @pl.when(h == rank)
            def _():
                for copy in map_keeps(h, rank):
                    copy.start()

        @pl.when(step == 1)
        def _():
            for copy in x_landing[:2]:
                copy.wait()
            for copy in x_second + z_first[0] + z_first[1] + [across[0][0], across[1][0]]:
                copy.start()

        @pl.when(step == HK // TOGETHER - 2)
        def _():
            for copy in x_landing[2:]:
                copy.wait()
            for copy in z_first[2] + [across[2][0]]:
                copy.start()

        return carry

    lax.fori_loop(0, HK // TOGETHER, key_heads, 0)

    for number in range(3):
        for copy in z_landing[number][:2]:
            copy.wait()
        for copy in z_second[number] + [across[number][3], across[number][1]]:
            copy.start()

    for copy in map_keeps(0, 0):
        copy.wait()
    prefix[0] = maps_in[0]
    prefix_add[0] = adds_in[0].astype(F32)

    def chain(index, carry):
        for copy in map_keeps(index, index):
            copy.wait()
        step = split(maps_in[index])
        prefix[index] = mm3(step, split(prefix[index - 1]))
        prefix_add[index] = mm3(step, split(prefix_add[index - 1])) + adds_in[index].astype(F32)
        return carry

    lax.fori_loop(1, GROUP, chain, 0)
    last_add[...] = prefix_add[GROUP - 1].astype(BF16)

    def group_copies(to, source):
        return [
            pltpu.make_async_remote_copy(
                src_ref=kept,
                dst_ref=target.at[source],
                send_sem=send2.at[number, to],
                recv_sem=recv2.at[number, source],
                device_id=device(to, rank),
                device_id_type=MESH,
            )
            for number, (kept, target) in enumerate([(prefix.at[GROUP - 1], groups_in), (last_add, groups_add)])
        ]

    def send_group(to, carry):
        for copy in group_copies(to, group):
            copy.start()
        return carry

    lax.fori_loop(group + 1, groups, send_group, 0)

    for number in range(3):
        for copy in z_landing[number][2:]:
            copy.wait()
        across[number][2].start()

    def enter(source, state):
        for copy in group_copies(group, source):
            copy.wait_recv()
        return mm3(split(groups_in[source]), split(state)) + groups_add[source].astype(F32)

    entering = split(lax.fori_loop(0, group, enter, jnp.zeros((DK, DV), F32)))

    def state_copy(to, head):
        return pltpu.make_async_remote_copy(
            src_ref=states.at[to],
            dst_ref=states_in.at[head],
            send_sem=send3.at[to],
            recv_sem=recv3.at[head],
            device_id=device(group, to),
            device_id_type=MESH,
        )

    def state_keep(to, head):
        return pltpu.make_async_copy(states.at[to], states_in.at[head], recv3.at[head])

    def give(to):
        @pl.when(to != rank)
        def _():
            state_copy(to, rank).start()

        @pl.when(to == rank)
        def _():
            state_keep(to, rank).start()

    states[0] = entering[0]
    give(0)

    def spread(index, carry):
        moved = mm3(split(prefix[index - 1]), entering) + prefix_add[index - 1]
        states[index] = moved.astype(BF16)
        give(index)
        return carry

    lax.fori_loop(1, GROUP, spread, 0)

    gain = gain_ref[...]
    loads[3].wait()

    def finish(h, carry):
        columns = pl.ds(pl.multiple_of(h * DV, DV), DV)
        gate = gate_ref[:, columns].astype(F32)
        scale = gain * (gate / (1.0 + jnp.exp(-gate)))
        state_keep(h, h).wait()
        state = states_in[h]
        out = local_out[h] + (mm(query_high[h], state) + mm(query_low[h], state))
        inv_rms = lax.rsqrt(jnp.sum(out * out, axis=1, keepdims=True) * (1.0 / DV) + 1e-6)
        core_out[:, columns] = (out * inv_rms * scale).astype(BF16)
        return carry

    lax.fori_loop(0, HV, finish, 0)

    loads[4].wait()
    loads[5].wait()
    for number in range(3):
        for copy in across_landing[number]:
            copy.wait()
    width = proj_hbm.shape[1]

    def project(index, square):
        columns = pl.ds(pl.multiple_of(index * width, width), width)
        mixed = mm(core_out[...], proj[index])
        hidden = (residual_ref[:, columns].astype(F32) + mixed).astype(BF16)
        hidden_ref[:, columns] = hidden
        wide = hidden.astype(F32)
        return square + jnp.sum(wide * wide, axis=1, keepdims=True)

    square = lax.fori_loop(0, exp_size, project, jnp.zeros((128, 1), F32))
    inv_rms = lax.rsqrt(square * (1.0 / D) + 1e-6)
    normed_ref[...] = (hidden_ref[...].astype(F32) * inv_rms * post_gain_ref[...]).astype(BF16)

    def drain(index, carry):
        @pl.when(index != rank)
        def _():
            for copy in map_copies(index, rank):
                copy.wait_send()
            state_copy(index, rank).wait_send()

        return carry

    lax.fori_loop(0, GROUP, drain, 0)

    def drain_group(to, carry):
        for copy in group_copies(to, group):
            copy.wait_send()
        return carry

    lax.fori_loop(group + 1, groups, drain_group, 0)
    for copy in x_first + x_second:
        copy.wait_send()
    for number in range(3):
        for copy in z_first[number] + z_second[number] + across[number]:
            copy.wait_send()


def mixer(query, key, value, gate, residual, proj, strength, rate, head_gain, post_gain, stride):
    seq_size, exp_size = lax.axis_size("seq"), lax.axis_size("exp")
    groups = seq_size * exp_size // GROUP
    tokens = query.shape[0]
    vmem = pl.BlockSpec(memory_space=pltpu.VMEM)
    hbm = pl.BlockSpec(memory_space=pl.ANY)
    square = (128, 128)
    return pl.pallas_call(
        partial(mixer_kernel, seq_size, exp_size, stride),
        out_shape=[jax.ShapeDtypeStruct((tokens, D), BF16)] * 2,
        in_specs=[hbm] * 6 + [vmem] * 4,
        out_specs=[vmem, vmem],
        scratch_shapes=[
            pltpu.VMEM(query.shape, BF16),
            pltpu.VMEM(key.shape, BF16),
            pltpu.VMEM(value.shape, BF16),
            pltpu.VMEM(gate.shape, BF16),
            pltpu.VMEM(residual.shape, BF16),
            pltpu.VMEM((exp_size,) + proj.shape, BF16),
            pltpu.VMEM(value.shape, BF16),
            pltpu.VMEM((HV, tokens), F32),
            pltpu.VMEM((HV,) + square, F32),
            pltpu.VMEM((HV,) + square, BF16),
            pltpu.VMEM((HV,) + square, BF16),
            pltpu.VMEM((HV,) + square, F32),
            pltpu.VMEM((HV,) + square, BF16),
            pltpu.VMEM((GROUP,) + square, F32),
            pltpu.VMEM((GROUP,) + square, BF16),
            pltpu.VMEM((GROUP,) + square, F32),
            pltpu.VMEM((GROUP,) + square, F32),
            pltpu.VMEM(square, BF16),
            pltpu.VMEM((groups,) + square, F32),
            pltpu.VMEM((groups,) + square, BF16),
            pltpu.VMEM((GROUP,) + square, BF16),
            pltpu.VMEM((HV,) + square, BF16),
            pltpu.SemaphoreType.DMA((6,)),
            pltpu.SemaphoreType.DMA((2, HV)),
            pltpu.SemaphoreType.DMA((2, GROUP)),
            pltpu.SemaphoreType.DMA((2, groups)),
            pltpu.SemaphoreType.DMA((2, groups)),
            pltpu.SemaphoreType.DMA((GROUP,)),
            pltpu.SemaphoreType.DMA((HV,)),
            pltpu.SemaphoreType.DMA((28,)),
            pltpu.SemaphoreType.DMA((28,)),
        ],
        compiler_params=pltpu.CompilerParams(
            collective_id=0, has_side_effects=True, vmem_limit_bytes=56 * 1024 * 1024
        ),
        cost_estimate=pl.CostEstimate(flops=8_000_000_000, bytes_accessed=4_000_000, transcendentals=0),
    )(
        query,
        key,
        value,
        gate,
        residual,
        proj,
        rate.T,
        strength.T,
        head_gain.reshape(1, DV),
        post_gain.reshape(1, D),
    )


def slot_tables(expert_ids, gate_weights, experts, capacity):
    tokens = expert_ids.shape[0]
    named = expert_ids.T[:, None, :] == jnp.arange(experts, dtype=jnp.int32)[None, :, None]
    weight = jnp.sum(jnp.where(named, gate_weights.T[:, None, :], 0.0), axis=0)
    chosen = jnp.any(named, axis=0)
    earlier = jnp.arange(tokens)[:, None] < jnp.arange(tokens)[None, :]
    before = jnp.dot(chosen.astype(BF16), earlier.astype(BF16), preferred_element_type=F32).astype(jnp.int32)
    before = jnp.where(chosen, before, -1)
    here = before[:, None, :] == jnp.arange(capacity, dtype=jnp.int32)[None, :, None]
    pick = here.astype(BF16).reshape(experts * capacity, tokens)
    mix = jnp.where(here, weight[:, None, :], 0.0).reshape(experts * capacity, tokens)
    return pick, mix


def shards(
    residual_in,
    query_input,
    key_input,
    value_input,
    out_gate,
    write_strength,
    decay_rate,
    head_gain,
    out_proj,
    post_gain,
    expert_ids,
    gate_weights,
    expert_gate,
    expert_up,
    expert_down,
):
    tokens = residual_in.shape[0]
    devices = lax.axis_size(("seq", "exp"))
    local_experts = expert_gate.shape[0]
    experts = local_experts * devices
    capacity = max(2, tokens * TOP * 8 // (5 * experts))
    pick, mix = slot_tables(expert_ids, gate_weights, experts, capacity)
    both_axes = ("seq", "exp")
    stride = lax.axis_size("seq") // 4
    hidden_state, normed = mixer(
        query_input,
        key_input,
        value_input,
        out_gate,
        residual_in,
        out_proj,
        write_strength,
        decay_rate,
        head_gain,
        post_gain,
        stride,
    )
    pick = pick.reshape(devices, local_experts, capacity, tokens)
    returned = []
    arrived = []
    for e in range(local_experts):
        send = jnp.dot(pick[:, e].reshape(devices * capacity, tokens), normed, preferred_element_type=F32).astype(BF16)
        send = send.reshape(devices, capacity, D)
        arrived.append(lax.all_to_all(send, both_axes, split_axis=0, concat_axis=0, tiled=True))
    for e in range(local_experts):
        block = arrived[e].reshape(devices * capacity, D)
        gate_part = jnp.dot(block, expert_gate[e], preferred_element_type=F32)
        up_part = jnp.dot(block, expert_up[e], preferred_element_type=F32)
        inner = (gate_part / (1.0 + jnp.exp(-gate_part)) * up_part).astype(BF16)
        result = jnp.dot(inner, expert_down[e], preferred_element_type=F32).astype(BF16)
        result = result.reshape(devices, capacity, D)
        returned.append(lax.all_to_all(result, both_axes, split_axis=0, concat_axis=0, tiled=True))
    mix_high = mix.astype(BF16)
    mix_low = (mix - mix_high.astype(F32)).astype(BF16)
    mix = jnp.concatenate([mix_high, mix_low], axis=1).reshape(devices, local_experts, capacity, 2 * tokens)
    routed = 0.0
    for e in range(local_experts):
        both = lax.dot_general(
            mix[:, e].reshape(devices * capacity, 2 * tokens),
            returned[e].reshape(devices * capacity, D),
            (((0,), (0,)), ((), ())),
            preferred_element_type=F32,
        )
        routed = routed + (both[:tokens] + both[tokens:])
    return (hidden_state.astype(F32) + routed).astype(BF16)


def solution(mesh):
    both = ("seq", "exp")
    placed = (
        P(both, None),
        P(both, None),
        P(both, None),
        P(both, None),
        P(both, None),
        P(both, None),
        P(both, None),
        P(),
        P(None, "exp"),
        P(),
        P(both, None),
        P(both, None),
        P(both, None, None),
        P(both, None, None),
        P(both, None, None),
    )
    return jax.shard_map(shards, mesh=mesh, in_specs=placed, out_specs=P(both, None), check_vma=False)
```

time: 397 us -> 337 us (0.85)
  blocking collectives: 107 us -> 0 us
  waiting for transfers between devices: 136 us -> 175 us
  starting transfers between devices: 5.37 us -> 34.9 us
  between operations: 13.5 us -> 0.12 us
  other arithmetic: 10.4 us -> 2.71 us
  local copies, waits for them, and re-layouts: 6.17 us -> 0.01 us
    all_to_all x1 -> x0, blocking collectives: 107 us -> none  [shards(): lax.all_to_all(send, ('seq', 'exp'), split_axis=0, concat_axis=0, tiled=T...]
    all_to_all x1 -> x4, waiting for transfers between devices: 102 us -> 175 us  [the longest x2 87.7 us: shards(): lax.all_to_all(send, both_axes, split_axis=0, concat_axis=0, tiled=True)]
    all_gather x1 -> x0, waiting for transfers between devices: 33.5 us -> none  [shards(): all_proj = lax.all_gather(out_proj, 'exp', axis=1, tiled=True)]
    all_to_all x1 -> x4, starting transfers between devices: 5.37 us -> 34.9 us  [the longest x2 24.8 us: shards(): lax.all_to_all(send, both_axes, split_axis=0, concat_axis=0, tiled=True)]
    reshape x1 -> x0, other arithmetic: 7.5 us -> none  [shards(): jnp.concatenate(results, axis=1)]
    unnamed x26 -> x8, local copies, waits for them, and re-layouts: 6.05 us -> 0.01 us
    dot_general x3 -> x4, matrix products: 13.2 us -> 14.4 us  [the longest x2 7.4 us: shards(): jnp.dot(pick[:, e].reshape(devices * capacity, tokens), normed, preferred...]
  transfers between devices with their start and end apart: 2 -> 4, of which waited for: 2 -> 4; matrix products, arithmetic and copies ran while one was open for 1% -> 11% of each run, Pallas kernels for 19% -> 0%
where the time goes in v2:
time: 337 us; the launch traced here: 336 us
  waiting for transfers between devices  175 us (52%)
  Pallas kernels  78.5 us (23%)
  matrix products  44.9 us (13%)
  starting transfers between devices  34.9 us (10%)
    all_to_all x2, waiting for transfers between devices, shards(): lax.all_to_all(send, both_axes, split_axis=0, concat_axis=0, tiled=True)  87.7 us
    all_to_all x2, waiting for transfers between devices, shards(): lax.all_to_all(result, both_axes, split_axis=0, concat_axis=0, tiled=True)  87.1 us
    pallas_call x1, Pallas kernels, mixer(): pl.pallas_call(partial(mixer_kernel, seq_size, exp_size, stride), out_sha...  78.5 us
    all_to_all x2, starting transfers between devices, shards(): lax.all_to_all(send, both_axes, split_axis=0, concat_axis=0, tiled=True)  24.8 us
    dot_general x2, matrix products, shards(): jnp.dot(inner, expert_down[e], preferred_element_type=F32).astype(BF16)  20 us
    dot_general x2, matrix products, shards(): gate_part = jnp.dot(block, expert_gate[e], preferred_element_type=F32)  10.4 us
    all_to_all x2, starting transfers between devices, shards(): lax.all_to_all(result, both_axes, split_axis=0, concat_axis=0, tiled=True)  10.1 us
    dot_general x2, matrix products, shards(): jnp.dot(pick[:, e].reshape(devices * capacity, tokens), normed, preferred...  7.4 us
  transfers between devices with their start and end apart: 4, of which 4 were waited for; matrix products, arithmetic and copies ran while one was open for 11% of the time, Pallas kernels for 0%

profile of v2, /device:TPU:1, one launch (start us, length us, event | category | flops | bytes accessed | tf_op | source)
XLA Modules:
  0.0 336.0 jit_solution(8805186775673380744)
XLA Ops:
  0.0 0.9 fusion.32
  0.9 0.2 fusion.41
  1.0 0.2 iota_compare_fusion.1
  1.2 78.5 %shard_map.145 = (bf16[128,2048]{1,0:T(8,128)(2,1)}, bf16[128,2048]{1,0:T(8,128)(2,1)}) custom-call(bf16[128,1024]{1,0:T(8,128)(2,1)} %q_hbm.1, bf16[128,1024]{1,0:T(8,128)(2,1)} %k_hbm.1, bf16[128,2048]{1,0:T(8,128)(2,1)} %v_hbm.1, bf16[128,2048]{1,0:T(8,128)(2,1)} %gate_hbm.1, bf16[128,2048]{1,0:T(8,128)(2,1)} %residual_hbm.1, bf16[2048,512]{1,0:T(8,128)(2,1)} %proj_hbm.1, ...), custom_call_target="tpu_custom_call" | custom-call | flops 8000000000 | bytes 4000000 | tf_op jit(solution)/shard_map/pallas_call | solution.py:487
  79.7 4.2 %convert_bitcast_fusion.1 = bf16[128,8,2048]{2,1,0:T(8,128)(2,1)} fusion(bf16[128,2048]{1,0:T(8,128)(2,1)} %get-tuple-element.8, pred[128,2,8,128]{3,2,1,0:T(8,128)(4,1)S(1)} %iota_compare_fusion.1), kind=kOutput, calls=%fused_computation.13 | convolution fusion | flops 538968064 | bytes 4849664 | tf_op jit(solution)/shard_map/dot_general | solution.py:599
  83.9 0.0 copy-start
  83.9 19.8 %all-to-all-start.2 = ((bf16[128,8,2048]{2,1,0:T(8,128)(2,1)}), bf16[128,8,2048]{2,1,0:T(8,128)(2,1)}, u32[]{:S(2)}, u32[]{:S(2)}) async-start(bf16[128,8,2048]{2,1,0:T(8,128)(2,1)} %convert_bitcast_fusion.1), calls=%async_computation.2 | async-start | bytes 8388608 | tf_op jit(solution)/shard_map/all_to_all | solution.py:601
  103.7 0.0 copy-done
  103.7 3.2 convert_bitcast_fusion.3
  106.9 49.8 %all-to-all-done.2 = bf16[128,8,2048]{2,1,0:T(8,128)(2,1)} async-done(((bf16[128,8,2048]{2,1,0:T(8,128)(2,1)}), bf16[128,8,2048]{2,1,0:T(8,128)(2,1)}, u32[]{:S(2)}, u32[]{:S(2)}) %all-to-all-start.2) | async-done | bytes 4194336 | tf_op jit(solution)/shard_map/all_to_all | solution.py:601
  156.7 5.0 %all-to-all-start = ((bf16[128,8,2048]{2,1,0:T(8,128)(2,1)}), bf16[128,8,2048]{2,1,0:T(8,128)(2,1)}, u32[]{:S(2)}, u32[]{:S(2)}) async-start(bf16[128,8,2048]{2,1,0:T(8,128)(2,1)} %convert_bitcast_fusion.3), calls=%async_computation | async-start | bytes 8388608 | tf_op jit(solution)/shard_map/all_to_all | solution.py:601
  161.8 5.2 %fusion.4 = f32[1024,512]{1,0:T(8,128)S(1)} fusion(bf16[128,8,2048]{2,1,0:T(8,128)(2,1)} %all-to-all-done.2, bf16[2,2048,512]{2,1,0:T(8,128)(2,1)} %param.27), kind=kOutput, calls=%fused_computation.4 | convolution fusion | flops 2147483648 | bytes 8388608 | tf_op jit(solution)/shard_map/dot_general | solution.py:604
  166.9 10.0 %convert_bitcast_fusion = bf16[128,8,2048]{2,1,0:T(8,128)(2,1)} fusion(bf16[2,512,2048]{2,1,0:T(8,128)(2,1)} %param.29, f32[1024,512]{1,0:T(8,128)S(1)} %fusion.4, bf16[2,2048,512]{2,1,0:T(8,128)(2,1)} %param.28, bf16[128,8,2048]{2,1,0:T(8,128)(2,1)} %all-to-all-done.2), kind=kOutput, calls=%fused_computation.12 | convolution fusion | flops 4299685888 | bytes 14680064 | tf_op jit(solution)/shard_map/dot_general | solution.py:607
  177.0 37.9 %all-to-all-done = bf16[128,8,2048]{2,1,0:T(8,128)(2,1)} async-done(((bf16[128,8,2048]{2,1,0:T(8,128)(2,1)}), bf16[128,8,2048]{2,1,0:T(8,128)(2,1)}, u32[]{:S(2)}, u32[]{:S(2)}) %all-to-all-start) | async-done | bytes 4194336 | tf_op jit(solution)/shard_map/all_to_all | solution.py:601
  214.9 5.0 %all-to-all-start.3 = ((bf16[128,8,2048]{2,1,0:T(8,128)(2,1)}), bf16[128,8,2048]{2,1,0:T(8,128)(2,1)}, u32[]{:S(2)}, u32[]{:S(2)}) async-start(bf16[128,8,2048]{2,1,0:T(8,128)(2,1)} %convert_bitcast_fusion), calls=%async_computation.3 | async-start | bytes 8388608 | tf_op jit(solution)/shard_map/all_to_all | solution.py:609
  219.9 5.2 %fusion.10 = f32[1024,512]{1,0:T(8,128)S(1)} fusion(bf16[128,8,2048]{2,1,0:T(8,128)(2,1)} %all-to-all-done, bf16[2,2048,512]{2,1,0:T(8,128)(2,1)} %param.27), kind=kOutput, calls=%fused_computation.10 | convolution fusion | flops 2147483648 | bytes 8388608 | tf_op jit(solution)/shard_map/dot_general | solution.py:604
  225.1 10.0 %convert_bitcast_fusion.2 = bf16[128,8,2048]{2,1,0:T(8,128)(2,1)} fusion(bf16[2,512,2048]{2,1,0:T(8,128)(2,1)} %param.29, f32[1024,512]{1,0:T(8,128)S(1)} %fusion.10, bf16[2,2048,512]{2,1,0:T(8,128)(2,1)} %param.28, bf16[128,8,2048]{2,1,0:T(8,128)(2,1)} %all-to-all-done), kind=kOutput, calls=%fused_computation.14 | convolution fusion | flops 4299685888 | bytes 14680064 | tf_op jit(solution)/shard_map/dot_general | solution.py:607
  235.1 0.0 copy-start.2
  235.1 0.0 copy-start.3
  235.1 38.0 %all-to-all-done.3 = bf16[128,8,2048]{2,1,0:T(8,128)(2,1)} async-done(((bf16[128,8,2048]{2,1,0:T(8,128)(2,1)}), bf16[128,8,2048]{2,1,0:T(8,128)(2,1)}, u32[]{:S(2)}, u32[]{:S(2)}) %all-to-all-start.3) | async-done | bytes 4194336 | tf_op jit(solution)/shard_map/all_to_all | solution.py:609
  273.1 5.0 %all-to-all-start.1 = ((bf16[128,8,2048]{2,1,0:T(8,128)(2,1)}), bf16[128,8,2048]{2,1,0:T(8,128)(2,1)}, u32[]{:S(2)}, u32[]{:S(2)}) async-start(bf16[128,8,2048]{2,1,0:T(8,128)(2,1)} %convert_bitcast_fusion.2), calls=%async_computation.1 | async-start | bytes 8388608 | tf_op jit(solution)/shard_map/all_to_all | solution.py:609
  278.1 0.0 copy-done.2
  278.1 0.0 copy-done.3
  278.1 0.1 select_reduce_fusion
  278.3 0.2 fusion.42
  278.5 0.2 select_convert_fusion
  278.6 3.5 %fusion = f32[256,2048]{1,0:T(8,128)S(1)} fusion(bf16[128,8,2048]{2,1,0:T(8,128)(2,1)} %all-to-all-done.3, bf16[128,2,8,128]{3,2,1,0:T(8,128)(2,1)S(1)} %fusion.42, bf16[128,2,8,128]{3,2,1,0:T(8,128)(2,1)S(1)} %select_convert_fusion), kind=kOutput, calls=%fused_computation | convolution fusion | flops 1074790400 | bytes 7340032 | tf_op jit(solution)/shard_map/dot_general | solution.py:615
  282.1 49.2 %all-to-all-done.1 = bf16[128,8,2048]{2,1,0:T(8,128)(2,1)} async-done(((bf16[128,8,2048]{2,1,0:T(8,128)(2,1)}), bf16[128,8,2048]{2,1,0:T(8,128)(2,1)}, u32[]{:S(2)}, u32[]{:S(2)}) %all-to-all-start.1) | async-done | bytes 4194336 | tf_op jit(solution)/shard_map/all_to_all | solution.py:609
  331.3 0.0 copy-start.1
  331.3 3.5 %fusion.6 = f32[256,2048]{1,0:T(8,128)S(1)} fusion(bf16[128,8,2048]{2,1,0:T(8,128)(2,1)} %all-to-all-done.1, bf16[128,2,8,128]{3,2,1,0:T(8,128)(2,1)S(1)} %select_convert_fusion, bf16[128,2,8,128]{3,2,1,0:T(8,128)(2,1)S(1)} %fusion.42), kind=kOutput, calls=%fused_computation.6 | convolution fusion | flops 1074790400 | bytes 7340032 | tf_op jit(solution)/shard_map/dot_general | solution.py:615
  334.8 0.0 copy-done.1
  334.8 1.2 fusion.45
Async XLA Ops:
  83.9 19.8 %copy-start = (bf16[128,2048]{1,0:T(8,128)(2,1)S(1)}, bf16[128,2048]{1,0:T(8,128)(2,1)}, u32[]{:S(2)}) copy-start(bf16[128,2048]{1,0:T(8,128)(2,1)} %get-tuple-element.8) | copy-start | bytes 1572868
  83.9 72.8 %all-to-all-start.2 = ((bf16[128,8,2048]{2,1,0:T(8,128)(2,1)}), bf16[128,8,2048]{2,1,0:T(8,128)(2,1)}, u32[]{:S(2)}, u32[]{:S(2)}) async-start(bf16[128,8,2048]{2,1,0:T(8,128)(2,1)} %convert_bitcast_fusion.1), calls=%async_computation.2 | async-start | bytes 8388608 | tf_op jit(solution)/shard_map/all_to_all | solution.py:601
  156.7 58.2 %all-to-all-start = ((bf16[128,8,2048]{2,1,0:T(8,128)(2,1)}), bf16[128,8,2048]{2,1,0:T(8,128)(2,1)}, u32[]{:S(2)}, u32[]{:S(2)}) async-start(bf16[128,8,2048]{2,1,0:T(8,128)(2,1)} %convert_bitcast_fusion.3), calls=%async_computation | async-start | bytes 8388608 | tf_op jit(solution)/shard_map/all_to_all | solution.py:601
  214.9 58.2 %all-to-all-start.3 = ((bf16[128,8,2048]{2,1,0:T(8,128)(2,1)}), bf16[128,8,2048]{2,1,0:T(8,128)(2,1)}, u32[]{:S(2)}, u32[]{:S(2)}) async-start(bf16[128,8,2048]{2,1,0:T(8,128)(2,1)} %convert_bitcast_fusion), calls=%async_computation.3 | async-start | bytes 8388608 | tf_op jit(solution)/shard_map/all_to_all | solution.py:609
  235.1 43.0 %copy-start.2 = (s32[128,10]{0,1:T(8,128)S(1)}, s32[128,10]{0,1:T(8,128)}, u32[]{:S(2)}) copy-start(s32[128,10]{0,1:T(8,128)} %param.25) | copy-start | bytes 15364
  235.1 43.0 %copy-start.3 = (f32[128,10]{0,1:T(8,128)S(1)}, f32[128,10]{0,1:T(8,128)}, u32[]{:S(2)}) copy-start(f32[128,10]{0,1:T(8,128)} %param.26) | copy-start | bytes 15364
  273.1 58.2 %all-to-all-start.1 = ((bf16[128,8,2048]{2,1,0:T(8,128)(2,1)}), bf16[128,8,2048]{2,1,0:T(8,128)(2,1)}, u32[]{:S(2)}, u32[]{:S(2)}) async-start(bf16[128,8,2048]{2,1,0:T(8,128)(2,1)} %convert_bitcast_fusion.2), calls=%async_computation.1 | async-start | bytes 8388608 | tf_op jit(solution)/shard_map/all_to_all | solution.py:609
  331.3 3.5 %copy-start.1 = (bf16[128,2048]{1,0:T(8,128)(2,1)S(1)}, bf16[128,2048]{1,0:T(8,128)(2,1)}, u32[]{:S(2)}) copy-start(bf16[128,2048]{1,0:T(8,128)(2,1)} %get-tuple-element.7) | copy-start | bytes 1572868
